TPU v7x, 32 devices: a whole 2x2x4 slice. The times are simulated.
32 devices in a mesh: wide: 8 (over y, x, core), narrow: 4 (over z).
Axes of the slice: x: 2, y: 2, z: 4, core: 2. Of those that a mesh axis runs over, the one named last changes fastest.
Arguments:
- hidden: bfloat16 [1024, 4096], P('wide', 'narrow'), may hold values from -6 to 6
- head_weight: bfloat16 [32768, 4096], P('wide', 'narrow'), may hold values from -0.25 to 0.25
- lse: float32 [1024], replicated, may hold values from 12 to 14
- targets: int32 [1024], replicated, may hold values from 0 to 32767
- loss_weight: float32 [1024], replicated, may hold values from 16 to 48
- block_tiles: int32 [8, 8, 4], P(None, 'wide'), may hold values from 0 to 31, as said below
- block_counts: int32 [8, 8], P(None, 'wide'), may hold values from 0 to 4, as said below
- gate_pre: bfloat16 [1024, 7168], P('wide', 'narrow'), may hold values from -6 to 6
- up_pre: bfloat16 [1024, 7168], P('wide', 'narrow'), may hold values from -6 to 6
- down_weight: bfloat16 [7168, 4096], P('narrow'), may hold values from -0.0625 to 0.0625
Outputs:
- head_grad: bfloat16 [1024, 4096], P('wide', 'narrow')
- gate_grad: bfloat16 [1024, 7168], P('wide', 'narrow')
- up_grad: bfloat16 [1024, 7168], P('wide', 'narrow')
Inputs may be any that keep to these rules, and one draw needn't show every extreme that they name: The first block_counts[b, s] entries of block_tiles[b, s] are distinct; the other entries are ignored. `block_counts`: some row block has 4 active tiles in some shard; one shard has exactly 16 active tiles over all row blocks, and no shard has more.
All inputs are finite; a program needn't handle non-finite values.
Results may differ from a plain program's by a relative error of at most 0.0035.
The roundings to bfloat16 on the way count: a program that leaves them out, or rounds other values in their place, can miss the bound.
Values may be sent and summed in bfloat16 or wider, within the bound.
No kernel may reach another device: no remote copies, remote signals or barrier semaphores. Data moves between devices by JAX's collectives and lax.ppermute only.
A program may use at most 128 MiB of HBM per device.

v0:
```python
import jax
import jax.numpy as jnp
from jax import lax
from jax.sharding import PartitionSpec as P

TILE = 128


def slot_table(tiles_here, counts_here, slot_count):
    block_total, per_block = tiles_here.shape
    slot_live = (jnp.arange(per_block, dtype=jnp.int32)[None, :] < counts_here[:, None]).reshape(-1)
    position = jnp.cumsum(slot_live.astype(jnp.int32)) - 1
    select = (position[None, :] == jnp.arange(slot_count, dtype=jnp.int32)[:, None]) & slot_live[
        None, :
    ]
    chosen = select.astype(jnp.int32)
    block_ids = jnp.repeat(jnp.arange(block_total, dtype=jnp.int32), per_block)
    slot_blocks = jnp.sum(chosen * block_ids[None, :], axis=1)
    slot_tiles = jnp.sum(chosen * tiles_here.reshape(-1)[None, :], axis=1)
    return (slot_blocks, slot_tiles, jnp.sum(chosen, axis=1) > 0)


def cell_weights(logits, lse_rows, scale_rows, slot_live):
    scaled = jnp.exp(logits - lse_rows[:, :, None]) * scale_rows[:, :, None]
    return jnp.where(slot_live[:, None, None], scaled, 0.0).astype(jnp.bfloat16)


def on_device(
    hidden,
    head_weight,
    lse,
    targets,
    loss_weight,
    block_tiles,
    block_counts,
    gate_pre,
    up_pre,
    down_weight,
):
    features = hidden.shape[1]
    row_count = hidden.shape[0]
    vocab_here = head_weight.shape[0]
    offset = lax.axis_index("wide") * vocab_here
    gathered = lax.all_gather(hidden, "wide", axis=0, tiled=True)
    blocks = gathered.shape[0] // TILE
    weight_tiles = head_weight.reshape(vocab_here // TILE, TILE, features)
    tiles_here = block_tiles[:, 0, :]
    counts_here = block_counts[:, 0]
    per_block = tiles_here.shape[1]
    lse_blocks = lse.reshape(blocks, TILE)
    scale_blocks = loss_weight.reshape(blocks, TILE)
    slot_count = blocks // 2 * per_block
    slot_blocks, slot_tiles, slot_live = slot_table(tiles_here, counts_here, slot_count)
    picked = jnp.take(weight_tiles, slot_tiles, axis=0)
    row_blocks = jnp.take(gathered.reshape(blocks, TILE, features), slot_blocks, axis=0)
    partial_value = jnp.einsum(
        "srd,scd->src", row_blocks, picked, preferred_element_type=jnp.float32
    )
    slot_lse = jnp.take(lse_blocks, slot_blocks, axis=0)
    slot_scale = jnp.take(scale_blocks, slot_blocks, axis=0)
    logits = lax.psum(partial_value, "narrow")
    cell_probs = cell_weights(logits, slot_lse, slot_scale, slot_live)
    contrib = jnp.einsum("src,scd->srd", cell_probs, picked, preferred_element_type=jnp.float32)
    contrib = contrib.reshape(slot_count, TILE * features)
    block_span = row_count * lax.axis_size("wide") // TILE
    wanted = jnp.arange(block_span, dtype=jnp.int32)
    member = ((slot_blocks[None, :] == wanted[:, None]) & slot_live[None, :]).astype(jnp.float32)
    softmax_part = jnp.dot(
        member, contrib, precision=lax.Precision.HIGHEST, preferred_element_type=jnp.float32
    ).reshape(row_count * lax.axis_size("wide"), features)
    local_ids = targets - offset
    inside = (local_ids >= 0) & (local_ids < vocab_here)
    target_rows = jnp.take(head_weight, jnp.clip(local_ids, 0, vocab_here - 1), axis=0).astype(
        jnp.float32
    )
    factor = jnp.where(inside, loss_weight, 0.0)
    head_grad = lax.psum_scatter(
        softmax_part - factor[:, None] * target_rows, "wide", scatter_dimension=0, tiled=True
    ).astype(jnp.bfloat16)
    unit_grad = lax.dot_general(
        lax.all_gather(head_grad, "narrow", axis=1, tiled=True),
        down_weight,
        (((1,), (1,)), ((), ())),
        preferred_element_type=jnp.float32,
    )
    gate_value = gate_pre.astype(jnp.float32)
    up_value = up_pre.astype(jnp.float32)
    gate_sig = jax.nn.sigmoid(gate_value)
    up_grad = (unit_grad * gate_value * gate_sig).astype(jnp.bfloat16)
    gate_grad = (unit_grad * up_value * gate_sig * (1.0 + gate_value * (1.0 - gate_sig))).astype(
        jnp.bfloat16
    )
    return (head_grad, gate_grad, up_grad)


def solution(mesh):
    in_specs = (
        P("wide", "narrow"),
        P("wide", "narrow"),
        P(),
        P(),
        P(),
        P(None, "wide", None),
        P(None, "wide"),
        P("wide", "narrow"),
        P("wide", "narrow"),
        P("narrow", None),
    )
    out_specs = (P("wide", "narrow"), P("wide", "narrow"), P("wide", "narrow"))
    return jax.shard_map(
        on_device, mesh=mesh, in_specs=in_specs, out_specs=out_specs, check_vma=False
    )
```

profile of v0, /device:TPU:0, one launch (start us, length us, event | category | flops | bytes accessed | tf_op | source)
XLA Modules:
  0.0 223.7 jit_solution(11905009591479860913)
XLA Ops:
  7.2 0.0 all-gather.3.cloned.1.call-start
  7.2 0.7 all-gather.3.cloned.1.call-update
  7.9 0.0 all-reduce.2.cloned.1.call-start
  8.0 0.7 iota_compare_fusion.2
  8.7 0.1 reshape.201
  8.8 0.1 lt.82
  8.9 0.1 mul.57
  8.9 0.8 copy.18
  9.7 0.1 mul.60
  9.8 0.1 reduce-window.8
  9.8 0.1 add_reduce_fusion
  10.0 0.2 convert_reduce_fusion
  10.1 0.6 gather_fusion.3
  10.7 1.2 gather_fusion.4
  12.0 6.1 %gather_fusion.1 = bf16[16,128,1024]{2,1,0:T(8,128)(2,1)} fusion(bf16[32,128,1024]{2,1,0:T(8,128)(2,1)} %bitcast.21, s32[1024]{0:T(1024)S(1)} %pad_clamp_fusion.1), kind=kCustom, calls=%fused_computation.3 | custom fusion | bytes 8388672 | tf_op jit(solution)/shard_map/jit(_take)/gather | solution.py:54
  18.1 22.3 %all-gather.3.cloned.1.call-done = bf16[1024,1024]{1,0:T(8,128)(2,1)} async-done(((bf16[128,1024]{1,0:T(8,128)(2,1)}), bf16[1024,1024]{1,0:T(8,128)(2,1)}) %all-gather.3.cloned.1.call-update) | async-done | bytes 2097168 | tf_op jit(solution)/shard_map/all_gather | solution.py:44
  40.4 4.4 %gather_fusion = bf16[16,128,1024]{2,1,0:T(8,128)(2,1)} fusion(bf16[8,128,1024]{2,1,0:T(8,128)(2,1)} %bitcast.24, s32[1024]{0:T(1024)S(1)} %pad_clamp_fusion.2), kind=kCustom, calls=%fused_computation.2 | custom fusion | bytes 8388672 | tf_op jit(solution)/shard_map/jit(_take)/gather | solution.py:55
  44.8 6.0 %fusion = f32[16,128,128]{2,1,0:T(8,128)} fusion(bf16[16,128,1024]{2,1,0:T(8,128)(2,1)} %gather_fusion, pred[16]{0:T(512)(128)(4,1)S(1)} %get-tuple-element.14, bf16[16,128,1024]{2,1,0:T(8,128)(2,1)} %gather_fusion.1, pred[16]{0:T(512)(128)(4,1)S(1)} %get-tuple-element.13), kind=kOutput, calls=%fused_computation.6 | convolution fusion | flops 541065216 | bytes 9437216 | tf_op jit(solution)/shard_map/srd,scd->src/dot_general | solution.py:56
  50.8 0.2 reduce-scatter.2.cloned.1.call-start
  51.1 9.4 %gather_fusion.2 = bf16[1024,1024]{1,0:T(8,128)(2,1)S(1)} fusion(bf16[4096,1024]{1,0:T(8,128)(2,1)} %param.13, s32[1024]{0:T(1024)S(1)} %fusion.21), kind=kCustom, calls=%fused_computation.4 | custom fusion | bytes 4198400 | tf_op jit(solution)/shard_map/jit(_take)/gather | solution.py:73
  60.6 0.1 broadcast_select_fusion.4
  60.7 42.2 %all-reduce.2.cloned.1.call-done = f32[16,128,128]{2,1,0:T(8,128)} async-done(((f32[16,128,128]{2,1,0:T(8,128)}), f32[16,128,128]{2,1,0:T(8,128)}) %all-reduce.2.cloned.1.call-update) | async-done | bytes 1048592 | tf_op jit(solution)/shard_map/psum | solution.py:61
  102.9 3.8 %fusion.4 = f32[16,128,1024]{2,1,0:T(8,128)S(1)} fusion(bf16[16,128,1024]{2,1,0:T(8,128)(2,1)} %gather_fusion.1, pred[16]{0:T(512)(128)(4,1)S(1)} %get-tuple-element.13, f32[16,128,128]{2,1,0:T(8,128)} %all-reduce.2.cloned.1.call-done, f32[16,128]{1,0:T(8,128)S(1)} %get-tuple-element.10, f32[16,128]{1,0:T(8,128)S(1)} %get-tuple-element.9, ...), kind=kOutput, calls=%fused_computation.11 | convolution fusion | flops 540016640 | bytes 13647904 | tf_op jit(solution)/shard_map/src,scd->srd/dot_general | solution.py:63
  106.7 4.9 %copy.19 = f32[2,8,128,1024]{3,1,2,0:T(8,128)S(1)} copy(f32[2,8,128,1024]{3,2,1,0:T(8,128)S(1)} %bitcast.22) | data formatting | bytes 16777216
  111.6 4.4 %fusion.19 = f32[8,131072]{1,0:T(8,128)} fusion(f32[16,131072]{1,0:T(8,128)S(1)} %bitcast.23, s32[16]{0:T(128)S(1)} %get-tuple-element.6, pred[16]{0:T(512)(128)(4,1)S(1)} %broadcast_compare_fusion), kind=kOutput, calls=%fused_computation.43 | convolution fusion | flops 201326848 | bytes 12582992 | tf_op jit(solution)/shard_map/dot_general | solution.py:68
  116.0 4.9 %reshape.152 = f32[1024,1024]{1,0:T(8,128)} reshape(f32[8,131072]{1,0:T(8,128)} %fusion.19) | data formatting | bytes 8388608 | tf_op jit(solution)/shard_map/reshape | solution.py:70
  120.9 4.1 %multiply_subtract_fusion = f32[1024,1024]{1,0:T(8,128)} fusion(f32[1024,1024]{1,0:T(8,128)} %reshape.152, bf16[1024,1024]{1,0:T(8,128)(2,1)S(1)} %gather_fusion.2, f32[1024]{0:T(1024)S(1)} %and_select_fusion, pred[1024]{0:T(1024)(128)(4,1)S(1)} %compare_and_fusion), kind=kLoop, calls=%fused_computation.5 | loop fusion | flops 4194304 | bytes 10490880 | tf_op jit(solution)/shard_map/sub | solution.py:78
  125.0 0.3 all-gather.5.cloned.1.call-start
  125.3 50.3 %reduce-scatter.2.cloned.1.call-done = f32[128,1024]{1,0:T(8,128)} async-done(((f32[1024,1024]{1,0:T(8,128)}), f32[128,1024]{1,0:T(8,128)}) %reduce-scatter.2.cloned.1.call-update) | async-done | bytes 524304 | tf_op jit(solution)/shard_map/reduce_scatter | solution.py:77
  175.6 1.8 convert_element_type.45
  177.4 28.2 %all-gather.5.cloned.1.call-done = bf16[128,4096]{1,0:T(8,128)(2,1)} async-done(((bf16[128,1024]{1,0:T(8,128)(2,1)}), bf16[128,4096]{1,0:T(8,128)(2,1)}) %all-gather.5.cloned.1.call-update) | async-done | bytes 1048592 | tf_op jit(solution)/shard_map/all_gather | solution.py:81
  205.6 11.5 %fusion.12 = (bf16[128,1792]{1,0:T(8,128)(2,1)}, bf16[128,1792]{1,0:T(8,128)(2,1)}) fusion(bf16[128,1792]{1,0:T(8,128)(2,1)S(1)} %copy-done.4, bf16[128,1792]{1,0:T(8,128)(2,1)S(1)} %copy-done.5, bf16[128,4096]{1,0:T(8,128)(2,1)} %all-gather.5.cloned.1.call-done, bf16[1792,4096]{1,0:T(8,128)(2,1)} %param.21), kind=kOutput, calls=%fused_computation.23 | convolution fusion | flops 1882488832 | bytes 17563648 | tf_op jit(solution)/shard_map/dot_general | solution.py:80
  (27 shorter events, 0.2 us)
Async XLA Ops:
  7.2 3.0 %copy-start = (f32[1024]{0:T(1024)S(1)}, f32[1024]{0:T(1024)}, u32[]{:S(2)}) copy-start(f32[1024]{0:T(1024)} %param.14) | copy-start | bytes 12292
  7.2 33.2 %all-gather.3.cloned.1.call-start = ((), (), s32[]{:S(2)}) async-start(), calls=%async_computation.1 | async-start | bytes 2359296 | tf_op jit(solution)/shard_map/all_gather | solution.py:44
  7.9 95.0 %all-reduce.2.cloned.1.call-start = ((), (), s32[]{:S(2)}) async-start(), calls=%async_computation.2 | async-start | bytes 2097152 | tf_op jit(solution)/shard_map/psum | solution.py:61
  44.8 6.3 %copy-start.3 = (s32[1024]{0:T(1024)S(1)}, s32[1024]{0:T(1024)}, u32[]{:S(2)}) copy-start(s32[1024]{0:T(1024)} %param.15) | copy-start | bytes 12292
  50.8 124.7 %reduce-scatter.2.cloned.1.call-start = ((), (), s32[]{:S(2)}) async-start(), calls=%async_computation.3 | async-start | bytes 4718592 | tf_op jit(solution)/shard_map/reduce_scatter | solution.py:77
  51.1 9.5 %copy-start.2 = (f32[1024]{0:T(1024)S(1)}, f32[1024]{0:T(1024)}, u32[]{:S(2)}) copy-start(f32[1024]{0:T(1024)} %param.16) | copy-start | bytes 12292
  125.0 80.6 %copy-start.4 = (bf16[128,1792]{1,0:T(8,128)(2,1)S(1)}, bf16[128,1792]{1,0:T(8,128)(2,1)}, u32[]{:S(2)}) copy-start(bf16[128,1792]{1,0:T(8,128)(2,1)} %param.19) | copy-start | bytes 1376260
  125.0 80.6 %copy-start.5 = (bf16[128,1792]{1,0:T(8,128)(2,1)S(1)}, bf16[128,1792]{1,0:T(8,128)(2,1)}, u32[]{:S(2)}) copy-start(bf16[128,1792]{1,0:T(8,128)(2,1)} %param.20) | copy-start | bytes 1376260
  125.0 80.6 %all-gather.5.cloned.1.call-start = ((), (), s32[]{:S(2)}) async-start(), calls=%async_computation.4 | async-start | bytes 1310720 | tf_op jit(solution)/shard_map/all_gather | solution.py:81
  205.6 11.5 %copy-start.1 = (f32[1024]{0:T(1024)S(1)}, f32[1024]{0:T(1024)}, u32[]{:S(2)}) copy-start(f32[1024]{0:T(1024)} %param.14) | copy-start | bytes 12292
Sparse Core Ops, SparseCore 0:
  9.9 30.4 all-gather.2
  50.9 51.8 all-reduce.1
  125.1 50.4 reduce-scatter.1
  177.6 27.9 all-gather.4
where the time goes:
time: 224 us
  waiting for transfers between devices  144 us (64%)
  local copies, waits for them, and re-layouts  32.6 us (15%)
  matrix products  25.8 us (12%)
  between operations  13.9 us (6%)
  other arithmetic  7.04 us (3%)
    reduce_scatter x1, waiting for transfers between devices, on_device(): lax.psum_scatter(softmax_part - factor[:, None] * target_rows, 'wide', sc...  50.3 us
    psum x1, waiting for transfers between devices, on_device(): logits = lax.psum(partial_value, 'narrow')  42.2 us
    all_gather x1, waiting for transfers between devices, on_device(): lax.all_gather(head_grad, 'narrow', axis=1, tiled=True)  28.2 us
    all_gather x1, waiting for transfers between devices, on_device(): gathered = lax.all_gather(hidden, 'wide', axis=0, tiled=True)  22.3 us
    dot_general x1, matrix products, on_device(): lax.dot_general(lax.all_gather(head_grad, 'narrow', axis=1, tiled=True),...  11.5 us
    gather x1, local copies, waits for them, and re-layouts, on_device(): jnp.take(head_weight, jnp.clip(local_ids, 0, vocab_here - 1), axis=0)  9.44 us
    gather x1, local copies, waits for them, and re-layouts, on_device(): picked = jnp.take(weight_tiles, slot_tiles, axis=0)  6.13 us
    dot_general x1, matrix products, on_device(): jnp.einsum('srd,scd->src', row_blocks, picked, preferred_element_type=jnp...  6 us
  transfers between devices with their start and end apart: 4, of which 4 were waited for; matrix products, arithmetic and copies ran while one was open for 9% of the time, Pallas kernels for 0%

commit v1 on v0

--- a/solution.py
+++ b/solution.py
@@ -58,7 +58,8 @@
     )
     slot_lse = jnp.take(lse_blocks, slot_blocks, axis=0)
     slot_scale = jnp.take(scale_blocks, slot_blocks, axis=0)
-    logits = lax.psum(partial_value, "narrow")
+    parts = lax.all_gather(partial_value, "narrow")
+    logits = jnp.sum(parts, axis=0)
     cell_probs = cell_weights(logits, slot_lse, slot_scale, slot_live)
     contrib = jnp.einsum("src,scd->srd", cell_probs, picked, preferred_element_type=jnp.float32)
     contrib = contrib.reshape(slot_count, TILE * features)

time: 224 us -> 254 us (1.13)
  waiting for transfers between devices: 144 us -> 172 us
  other arithmetic: 7.04 us -> 9.67 us
    all_gather x0 -> x1, waiting for transfers between devices: none -> 69.9 us  [on_device(): parts = lax.all_gather(partial_value, 'narrow')]
    psum x1 -> x0, waiting for transfers between devices: 42.2 us -> none  [on_device(): logits = lax.psum(partial_value, 'narrow')]
    reduce_sum x0 -> x1, other arithmetic: none -> 2.64 us  [on_device(): logits = jnp.sum(parts, axis=0)]
  transfers between devices with their start and end apart: 4 -> 4, of which waited for: 4 -> 4; matrix products, arithmetic and copies ran while one was open for 9% -> 7% of each run, Pallas kernels for 0% -> 0%
where the time goes in v1:
time: 254 us
  waiting for transfers between devices  172 us (68%)
  local copies, waits for them, and re-layouts  32 us (13%)
  matrix products  25.2 us (10%)
  between operations  13.9 us (5%)
  other arithmetic  9.67 us (4%)
    all_gather x1, waiting for transfers between devices, on_device(): parts = lax.all_gather(partial_value, 'narrow')  69.9 us
    reduce_scatter x1, waiting for transfers between devices, on_device(): lax.psum_scatter(softmax_part - factor[:, None] * target_rows, 'wide', sc...  49.5 us
    all_gather x1, waiting for transfers between devices, on_device(): lax.all_gather(head_grad, 'narrow', axis=1, tiled=True)  28.2 us
    all_gather x1, waiting for transfers between devices, on_device(): gathered = lax.all_gather(hidden, 'wide', axis=0, tiled=True)  24.1 us
    dot_general x1, matrix products, on_device(): lax.dot_general(lax.all_gather(head_grad, 'narrow', axis=1, tiled=True),...  11.5 us
    gather x1, local copies, waits for them, and re-layouts, on_device(): jnp.take(head_weight, jnp.clip(local_ids, 0, vocab_here - 1), axis=0)  9.44 us
    gather x1, local copies, waits for them, and re-layouts, on_device(): picked = jnp.take(weight_tiles, slot_tiles, axis=0)  6.13 us
    dot_general x1, matrix products, on_device(): jnp.einsum('srd,scd->src', row_blocks, picked, preferred_element_type=jnp...  6.01 us
  transfers between devices with their start and end apart: 4, of which 4 were waited for; matrix products, arithmetic and copies ran while one was open for 7% of the time, Pallas kernels for 0%

profile of v1, /device:TPU:0, one launch (start us, length us, event | category | flops | bytes accessed | tf_op | source)
XLA Modules:
  0.0 253.7 jit_solution(13107658467184058478)
XLA Ops:
  7.2 0.7 all-gather.5.cloned.1.call-update
  7.9 0.0 all-gather.9.cloned.1.call-start
  8.0 0.7 iota_compare_fusion.2
  8.7 0.1 reshape.202
  8.8 0.1 lt.82
  8.9 0.1 mul.57
  8.9 0.8 copy.20
  9.7 0.1 mul.60
  9.8 0.1 reduce-window.8
  9.8 0.1 add_reduce_fusion
  9.9 0.2 convert_reduce_fusion
  10.1 6.1 %gather_fusion.1 = bf16[16,128,1024]{2,1,0:T(8,128)(2,1)} fusion(bf16[32,128,1024]{2,1,0:T(8,128)(2,1)} %bitcast.22, s32[1024]{0:T(1024)S(1)} %pad_clamp_fusion.1), kind=kCustom, calls=%fused_computation.3 | custom fusion | bytes 8388672 | tf_op jit(solution)/shard_map/jit(_take)/gather | solution.py:54
  16.3 24.1 %all-gather.5.cloned.1.call-done = bf16[1024,1024]{1,0:T(8,128)(2,1)} async-done(((bf16[128,1024]{1,0:T(8,128)(2,1)}), bf16[1024,1024]{1,0:T(8,128)(2,1)}) %all-gather.5.cloned.1.call-update) | async-done | bytes 2097168 | tf_op jit(solution)/shard_map/all_gather | solution.py:44
  40.4 4.4 %gather_fusion = bf16[16,128,1024]{2,1,0:T(8,128)(2,1)} fusion(bf16[8,128,1024]{2,1,0:T(8,128)(2,1)} %bitcast.25, s32[1024]{0:T(1024)S(1)} %pad_clamp_fusion.2), kind=kCustom, calls=%fused_computation.2 | custom fusion | bytes 8388672 | tf_op jit(solution)/shard_map/jit(_take)/gather | solution.py:55
  44.8 6.0 %fusion = f32[16,128,128]{2,1,0:T(8,128)} fusion(bf16[16,128,1024]{2,1,0:T(8,128)(2,1)} %gather_fusion, pred[16]{0:T(512)(128)(4,1)S(1)} %get-tuple-element.14, bf16[16,128,1024]{2,1,0:T(8,128)(2,1)} %gather_fusion.1, pred[16]{0:T(512)(128)(4,1)S(1)} %get-tuple-element.13), kind=kOutput, calls=%fused_computation.6 | convolution fusion | flops 541065216 | bytes 9437216 | tf_op jit(solution)/shard_map/srd,scd->src/dot_general | solution.py:56
  50.8 0.2 reduce-scatter.2.cloned.1.call-start
  51.1 0.6 gather_fusion.3
  51.7 0.6 gather_fusion.4
  52.3 9.4 %gather_fusion.2 = bf16[1024,1024]{1,0:T(8,128)(2,1)S(1)} fusion(bf16[4096,1024]{1,0:T(8,128)(2,1)} %param.13, s32[1024]{0:T(1024)S(1)} %fusion.21), kind=kCustom, calls=%fused_computation.4 | custom fusion | bytes 4198400 | tf_op jit(solution)/shard_map/jit(_take)/gather | solution.py:74
  61.8 0.1 broadcast_select_fusion.4
  61.8 69.9 %all-gather.9.cloned.1.call-done = f32[64,128,128]{2,1,0:T(8,128)} async-done(((f32[16,128,128]{2,1,0:T(8,128)}), f32[64,128,128]{2,1,0:T(8,128)}) %all-gather.9.cloned.1.call-update) | async-done | bytes 4194320 | tf_op jit(solution)/shard_map/all_gather | solution.py:61
  131.7 2.6 %reduce_sum.45 = f32[16,128,128]{2,1,0:T(8,128)S(1)} reduce(f32[4,16,128,128]{3,2,1,0:T(8,128)} %bitcast.26, f32[]{:T(128)} %constant.72.clone.1), dimensions={0}, to_apply=%region_4.5 | reduce | flops 786432 | bytes 5242884 | tf_op jit(solution)/shard_map/reduce_sum | solution.py:62
  134.4 3.2 %fusion.4 = f32[16,128,1024]{2,1,0:T(8,128)S(1)} fusion(bf16[16,128,1024]{2,1,0:T(8,128)(2,1)} %gather_fusion.1, pred[16]{0:T(512)(128)(4,1)S(1)} %get-tuple-element.13, f32[16,128,128]{2,1,0:T(8,128)S(1)} %reduce_sum.45, f32[16,128]{1,0:T(8,128)S(1)} %get-tuple-element.10, f32[16,128]{1,0:T(8,128)S(1)} %get-tuple-element.9, ...), kind=kOutput, calls=%fused_computation.11 | convolution fusion | flops 540016640 | bytes 13647904 | tf_op jit(solution)/shard_map/src,scd->srd/dot_general | solution.py:64
  137.6 4.9 %copy.21 = f32[2,8,128,1024]{3,1,2,0:T(8,128)S(1)} copy(f32[2,8,128,1024]{3,2,1,0:T(8,128)S(1)} %bitcast.23) | data formatting | bytes 16777216
  142.4 4.4 %fusion.19 = f32[8,131072]{1,0:T(8,128)} fusion(f32[16,131072]{1,0:T(8,128)S(1)} %bitcast.24, s32[16]{0:T(128)S(1)} %get-tuple-element.6, pred[16]{0:T(512)(128)(4,1)S(1)} %broadcast_compare_fusion), kind=kOutput, calls=%fused_computation.43 | convolution fusion | flops 201326848 | bytes 12582992 | tf_op jit(solution)/shard_map/dot_general | solution.py:69
  146.9 4.9 %reshape.152 = f32[1024,1024]{1,0:T(8,128)} reshape(f32[8,131072]{1,0:T(8,128)} %fusion.19) | data formatting | bytes 8388608 | tf_op jit(solution)/shard_map/reshape | solution.py:71
  151.8 4.1 %multiply_subtract_fusion = f32[1024,1024]{1,0:T(8,128)} fusion(f32[1024,1024]{1,0:T(8,128)} %reshape.152, bf16[1024,1024]{1,0:T(8,128)(2,1)S(1)} %gather_fusion.2, f32[1024]{0:T(1024)S(1)} %and_select_fusion, pred[1024]{0:T(1024)(128)(4,1)S(1)} %compare_and_fusion), kind=kLoop, calls=%fused_computation.5 | loop fusion | flops 4194304 | bytes 10490880 | tf_op jit(solution)/shard_map/sub | solution.py:79
  155.9 0.3 all-gather.7.cloned.1.call-start
  156.1 49.5 %reduce-scatter.2.cloned.1.call-done = f32[128,1024]{1,0:T(8,128)} async-done(((f32[1024,1024]{1,0:T(8,128)}), f32[128,1024]{1,0:T(8,128)}) %reduce-scatter.2.cloned.1.call-update) | async-done | bytes 524304 | tf_op jit(solution)/shard_map/reduce_scatter | solution.py:78
  205.7 1.8 convert_element_type.45
  207.5 28.2 %all-gather.7.cloned.1.call-done = bf16[128,4096]{1,0:T(8,128)(2,1)} async-done(((bf16[128,1024]{1,0:T(8,128)(2,1)}), bf16[128,4096]{1,0:T(8,128)(2,1)}) %all-gather.7.cloned.1.call-update) | async-done | bytes 1048592 | tf_op jit(solution)/shard_map/all_gather | solution.py:82
  235.7 11.5 %fusion.12 = (bf16[128,1792]{1,0:T(8,128)(2,1)}, bf16[128,1792]{1,0:T(8,128)(2,1)}) fusion(bf16[128,1792]{1,0:T(8,128)(2,1)S(1)} %copy-done.4, bf16[128,1792]{1,0:T(8,128)(2,1)S(1)} %copy-done.5, bf16[128,4096]{1,0:T(8,128)(2,1)} %all-gather.7.cloned.1.call-done, bf16[1792,4096]{1,0:T(8,128)(2,1)} %param.21), kind=kOutput, calls=%fused_computation.23 | convolution fusion | flops 1882488832 | bytes 17563648 | tf_op jit(solution)/shard_map/dot_general | solution.py:81
  (28 shorter events, 0.2 us)
Async XLA Ops:
  7.2 43.9 %copy-start = (f32[1024]{0:T(1024)S(1)}, f32[1024]{0:T(1024)}, u32[]{:S(2)}) copy-start(f32[1024]{0:T(1024)} %param.14) | copy-start | bytes 12292
  7.2 33.2 %all-gather.5.cloned.1.call-start = ((), (), s32[]{:S(2)}) async-start(), calls=%async_computation.1 | async-start | bytes 2359296 | tf_op jit(solution)/shard_map/all_gather | solution.py:44
  7.9 123.8 %all-gather.9.cloned.1.call-start = ((), (), s32[]{:S(2)}) async-start(), calls=%async_computation.4 | async-start | bytes 5242880 | tf_op jit(solution)/shard_map/all_gather | solution.py:61
  44.8 6.9 %copy-start.2 = (f32[1024]{0:T(1024)S(1)}, f32[1024]{0:T(1024)}, u32[]{:S(2)}) copy-start(f32[1024]{0:T(1024)} %param.16) | copy-start | bytes 12292
  44.8 7.5 %copy-start.3 = (s32[1024]{0:T(1024)S(1)}, s32[1024]{0:T(1024)}, u32[]{:S(2)}) copy-start(s32[1024]{0:T(1024)} %param.15) | copy-start | bytes 12292
  50.8 154.8 %reduce-scatter.2.cloned.1.call-start = ((), (), s32[]{:S(2)}) async-start(), calls=%async_computation.2 | async-start | bytes 4718592 | tf_op jit(solution)/shard_map/reduce_scatter | solution.py:78
  155.8 79.8 %copy-start.4 = (bf16[128,1792]{1,0:T(8,128)(2,1)S(1)}, bf16[128,1792]{1,0:T(8,128)(2,1)}, u32[]{:S(2)}) copy-start(bf16[128,1792]{1,0:T(8,128)(2,1)} %param.19) | copy-start | bytes 1376260
  155.8 79.8 %copy-start.5 = (bf16[128,1792]{1,0:T(8,128)(2,1)S(1)}, bf16[128,1792]{1,0:T(8,128)(2,1)}, u32[]{:S(2)}) copy-start(bf16[128,1792]{1,0:T(8,128)(2,1)} %param.20) | copy-start | bytes 1376260
  155.9 79.8 %all-gather.7.cloned.1.call-start = ((), (), s32[]{:S(2)}) async-start(), calls=%async_computation.3 | async-start | bytes 1310720 | tf_op jit(solution)/shard_map/all_gather | solution.py:82
  235.7 11.5 %copy-start.1 = (f32[1024]{0:T(1024)S(1)}, f32[1024]{0:T(1024)}, u32[]{:S(2)}) copy-start(f32[1024]{0:T(1024)} %param.14) | copy-start | bytes 12292
Sparse Core Ops, SparseCore 0:
  9.9 30.4 all-gather.4
  51.0 80.7 all-gather.8
  156.0 49.6 reduce-scatter.1
  207.7 27.9 all-gather.6
